TPU v7x, 32 devices: a whole 2x2x4 slice. The times are simulated.
32 devices in a mesh: row: 4 (over x, core), col: 8 (over z, y).
Axes of the slice: x: 2, y: 2, z: 4, core: 2. Of those that a mesh axis runs over, the one named last changes fastest.
Arguments:
- weight: bfloat16 [8192, 16384], P('row', 'col'), may hold values from -6 to 6
- gradient: bfloat16 [8192, 16384], P('row', 'col'), may hold values from -6 to 6
- old_basis: bfloat16 [8192, 1024], P('row'), may hold values from -0.0625 to 0.0625
- new_basis: bfloat16 [8192, 1024], P('row'), may hold values from -0.0625 to 0.0625
- first_moment: float32 [1024, 16384], P(None, ('col', 'row')), may hold values from -6 to 6
- second_moment: float32 [1024, 16384], P(None, ('col', 'row')), may hold values from 0.05 to 2
Outputs:
- new_weight: bfloat16 [8192, 16384], P('row', 'col')
- update: bfloat16 [8192, 16384], P('row', 'col')
- first_new: float32 [1024, 16384], P(None, ('col', 'row'))
- second_new: float32 [1024, 16384], P(None, ('col', 'row'))
All inputs are finite; a program needn't handle non-finite values.
Results may differ from a plain program's by a relative error of at most 0.0047.
Values may be sent and summed in bfloat16 or wider, within the bound.
A program may use at most 128 MiB of HBM per device.

v0:
```python
import jax
import jax.numpy as jnp
from jax import lax
from jax.sharding import PartitionSpec as P

beta_first = 0.9
beta_second = 0.95
epsilon = 1e-08
step_rate = 0.0025


def shards(columns, weight, gradient, old_basis, new_basis, first_moment, second_moment):
    part = old_basis.shape[1] // columns
    mine = lax.dynamic_slice_in_dim(old_basis, lax.axis_index("col") * part, part, axis=1)
    partial_sums = jnp.einsum("mr,mn->rn", new_basis, gradient, preferred_element_type=jnp.float32)
    projected = lax.psum_scatter(
        partial_sums.astype(jnp.bfloat16), "row", scatter_dimension=1, tiled=True
    )
    local_term = jnp.einsum("mc,mr->cr", mine, new_basis, preferred_element_type=jnp.float32)
    flipped = lax.all_gather(
        lax.psum(local_term, "row").astype(jnp.bfloat16), "col", axis=0, tiled=True
    )
    squares = jnp.square(flipped.astype(jnp.float32)).astype(jnp.bfloat16)
    moved_first = jnp.einsum(
        "cr,cn->rn", flipped, first_moment.astype(jnp.bfloat16), preferred_element_type=jnp.float32
    )
    moved_second = jnp.einsum(
        "cr,cn->rn", squares, second_moment.astype(jnp.bfloat16), preferred_element_type=jnp.float32
    )
    projected = projected.astype(jnp.float32)
    first_new = beta_first * moved_first + (1.0 - beta_first) * projected
    second_new = beta_second * moved_second + (1.0 - beta_second) * projected * projected
    direction = (first_new / (jnp.sqrt(second_new) + epsilon)).astype(jnp.bfloat16)
    back = jnp.dot(
        new_basis,
        lax.all_gather(direction, "row", axis=1, tiled=True),
        preferred_element_type=jnp.float32,
    )
    new_weight = (weight.astype(jnp.float32) - step_rate * back).astype(jnp.bfloat16)
    return (new_weight, back.astype(jnp.bfloat16), first_new, second_new)


def solution(mesh):
    placed = (
        P("row", "col"),
        P("row", "col"),
        P("row", None),
        P("row", None),
        P(None, ("col", "row")),
        P(None, ("col", "row")),
    )
    return jax.shard_map(
        lambda *blocks: shards(mesh.shape["col"], *blocks),
        mesh=mesh,
        in_specs=placed,
        out_specs=(
            P("row", "col"),
            P("row", "col"),
            P(None, ("col", "row")),
            P(None, ("col", "row")),
        ),
        check_vma=False,
    )
```

profile of v0, /device:TPU:0, one launch (start us, length us, event | category | flops | bytes accessed | tf_op | source)
XLA Modules:
  0.0 180.3 jit_solution(14779904578282714229)
XLA Ops:
  8.0 0.0 all-gather.3.cloned.1.call-start
  8.0 3.1 %fusion.6 = f32[128,1024]{1,0:T(8,128)S(1)} fusion(bf16[2048,1024]{1,0:T(8,128)(2,1)} %param.9, bf16[2048,1024]{1,0:T(8,128)(2,1)} %param.8, s32[]{:T(128)S(6)} %select_n.3), kind=kOutput, calls=%fused_computation.13 | convolution fusion | flops 536870912 | bytes 5242884 | tf_op jit(solution)/shard_map/mc,mr->cr/dot_general | solution.py:19
  11.2 19.1 %all-reduce.1 = bf16[128,1024]{1,0:T(8,128)(2,1)} all-reduce(f32[128,1024]{1,0:T(8,128)S(1)} %fusion.6), channel_id=1, replica_groups=mesh['row'=4,'col'=8] {'row'}, use_global_device_ids=true, to_apply=%region_0.0 | all-reduce | flops 131072 | bytes 786432 | tf_op jit(solution)/shard_map/psum | solution.py:21
  30.2 0.0 all-gather.3.cloned.1.call-update
  30.3 0.0 reduce-scatter.2.cloned.1.call-start
  30.3 14.0 %convolution_convert_fusion = bf16[1024,2048]{1,0:T(8,128)(2,1)} fusion(bf16[2048,1024]{1,0:T(8,128)(2,1)} %param.9, bf16[2048,2048]{1,0:T(8,128)(2,1)} %param.7), kind=kOutput, calls=%fused_computation.4 | convolution fusion | flops 8592031744 | bytes 16777216 | tf_op jit(solution)/shard_map/mr,mn->rn/dot_general | solution.py:15
  44.3 0.0 copy-start
  44.3 0.0 reduce-scatter.2.cloned.1.call-update
  44.3 0.2 all-gather.5.cloned.1.call-start
  44.6 35.5 %all-gather.3.cloned.1.call-done = bf16[1024,1024]{1,0:T(8,128)(2,1)} async-done(((bf16[128,1024]{1,0:T(8,128)(2,1)}), bf16[1024,1024]{1,0:T(8,128)(2,1)}) %all-gather.3.cloned.1.call-update) | async-done | bytes 2097168 | tf_op jit(solution)/shard_map/all_gather | solution.py:20
  80.1 9.2 %reduce-scatter.2.cloned.1.call-done = bf16[1024,512]{1,0:T(8,128)(2,1)} async-done(((bf16[1024,2048]{1,0:T(8,128)(2,1)}), bf16[1024,512]{1,0:T(8,128)(2,1)}) %reduce-scatter.2.cloned.1.call-update) | async-done | bytes 1048592 | tf_op jit(solution)/shard_map/reduce_scatter | solution.py:16
  89.3 0.0 copy-done
  89.3 0.0 copy-start.1
  89.3 0.0 copy-start.2
  89.3 0.0 copy-start.3
  89.3 3.3 %fusion.2 = f32[1024,512]{1,0:T(8,128)S(1)} fusion(bf16[1024,512]{1,0:T(8,128)(2,1)} %reduce-scatter.2.cloned.1.call-done, bf16[1024,1024]{1,0:T(8,128)(2,1)} %all-gather.3.cloned.1.call-done, f32[1024,512]{1,0:T(8,128)S(1)} %copy-done), kind=kOutput, calls=%fused_computation.8 | convolution fusion | flops 1080033280 | bytes 7340032 | tf_op jit(solution)/shard_map/cr,cn->rn/dot_general | solution.py:27
  92.7 0.0 copy-done.1
  92.7 0.0 copy-done.2
  92.7 0.1 copy-done.3
  92.8 0.0 copy-start.4
  92.8 3.6 %divide_convert_fusion = (bf16[1024,512]{1,0:T(8,128)(2,1)}, f32[1024,512]{1,0:T(8,128)}) fusion(f32[1024,512]{1,0:T(8,128)S(1)} %fusion.2, bf16[1024,512]{1,0:T(8,128)(2,1)S(1)} %copy-done.3, bf16[1024,1024]{1,0:T(8,128)(2,1)S(1)} %copy-done.2, f32[1024,512]{1,0:T(8,128)S(1)} %copy-done.1), kind=kOutput, calls=%fused_computation.10 | convolution fusion | flops 1077936128 | bytes 10485760 | tf_op jit(solution)/shard_map/cr,cn->rn/dot_general | solution.py:24
  96.3 0.0 copy-done.4
  96.3 0.0 all-gather.5.cloned.1.call-update
  96.4 12.4 %copy.10 = bf16[2048,2048]{0,1:T(8,128)(2,1)} copy(bf16[2048,2048]{1,0:T(8,128)(2,1)} %param.6) | data formatting | bytes 16777216 | tf_op args[0]
  108.7 22.1 %all-gather.5.cloned.1.call-done = bf16[1024,2048]{1,0:T(8,128)(2,1)} async-done(((bf16[1024,512]{1,0:T(8,128)(2,1)}), bf16[1024,2048]{1,0:T(8,128)(2,1)}) %all-gather.5.cloned.1.call-update) | async-done | bytes 4194320 | tf_op jit(solution)/shard_map/all_gather | solution.py:36
  130.8 17.6 %fusion = (bf16[2048,2048]{0,1:T(8,128)(2,1)}, bf16[2048,2048]{1,0:T(8,128)(2,1)}) fusion(bf16[2048,2048]{0,1:T(8,128)(2,1)} %copy.10, bf16[1024,2048]{1,0:T(8,128)(2,1)} %all-gather.5.cloned.1.call-done, bf16[2048,1024]{1,0:T(8,128)(2,1)} %param.9), kind=kOutput, calls=%fused_computation.1 | convolution fusion | flops 8610906112 | bytes 33554432 | tf_op jit(solution)/shard_map/dot_general | solution.py:34
  148.4 12.2 %copy.11 = bf16[2048,2048]{1,0:T(8,128)(2,1)} copy(bf16[2048,2048]{0,1:T(8,128)(2,1)} %get-tuple-element.10) | data formatting | bytes 16777216
  160.6 12.2 %copy.12 = bf16[2048,2048]{1,0:T(8,128)(2,1)} copy(bf16[2048,2048]{0,1:T(8,128)(2,1)} %bitcast.13) | data formatting | bytes 16777216
Async XLA Ops:
  8.0 72.1 %all-gather.3.cloned.1.call-start = ((), (), s32[]{:S(2)}) async-start(), calls=%async_computation.1 | async-start | bytes 2359296 | tf_op jit(solution)/shard_map/all_gather | solution.py:20
  30.3 59.1 %reduce-scatter.2.cloned.1.call-start = ((), (), s32[]{:S(2)}) async-start(), calls=%async_computation.2 | async-start | bytes 5242880 | tf_op jit(solution)/shard_map/reduce_scatter | solution.py:16
  44.3 45.0 %copy-start = (f32[1024,512]{1,0:T(8,128)S(1)}, f32[1024,512]{1,0:T(8,128)}, u32[]{:S(2)}) copy-start(f32[1024,512]{1,0:T(8,128)} %param.11) | copy-start | bytes 6291460
  44.3 86.5 %all-gather.5.cloned.1.call-start = ((), (), s32[]{:S(2)}) async-start(), calls=%async_computation.3 | async-start | bytes 5242880 | tf_op jit(solution)/shard_map/all_gather | solution.py:36
  89.3 3.3 %copy-start.1 = (f32[1024,512]{1,0:T(8,128)S(1)}, f32[1024,512]{1,0:T(8,128)}, u32[]{:S(2)}) copy-start(f32[1024,512]{1,0:T(8,128)} %param.10) | copy-start | bytes 6291460
  89.3 3.3 %copy-start.2 = (bf16[1024,1024]{1,0:T(8,128)(2,1)S(1)}, bf16[1024,1024]{1,0:T(8,128)(2,1)}, u32[]{:S(2)}) copy-start(bf16[1024,1024]{1,0:T(8,128)(2,1)} %all-gather.3.cloned.1.call-done) | copy-start | bytes 6291460
  89.3 3.4 %copy-start.3 = (bf16[1024,512]{1,0:T(8,128)(2,1)S(1)}, bf16[1024,512]{1,0:T(8,128)(2,1)}, u32[]{:S(2)}) copy-start(bf16[1024,512]{1,0:T(8,128)(2,1)} %reduce-scatter.2.cloned.1.call-done) | copy-start | bytes 3145732
  92.8 3.6 %copy-start.4 = (f32[1024,512]{1,0:T(8,128)}, f32[1024,512]{1,0:T(8,128)S(1)}, u32[]{:S(2)}) copy-start(f32[1024,512]{1,0:T(8,128)S(1)} %fusion.2) | copy-start | bytes 6291460
Sparse Core Ops, SparseCore 0:
  30.4 49.6 all-gather.2
Sparse Core Ops, SparseCore 1:
  44.4 44.8 reduce-scatter.1
  96.5 34.3 all-gather.4
where the time goes:
time: 181 us; the launch traced here: 180 us
  waiting for transfers between devices  66.9 us (37%)
  matrix products  41.6 us (23%)
  local copies, waits for them, and re-layouts  36.9 us (20%)
  blocking collectives  19.1 us (11%)
  between operations  15.5 us (9%)
    unnamed x13, local copies, waits for them, and re-layouts  36.9 us
    all_gather x1, waiting for transfers between devices, shards(): lax.all_gather(lax.psum(local_term, 'row').astype(jnp.bfloat16), 'col', a...  35.5 us
    all_gather x1, waiting for transfers between devices, shards(): lax.all_gather(direction, 'row', axis=1, tiled=True)  22.1 us
    psum x1, blocking collectives, shards(): lax.psum(local_term, 'row').astype(jnp.bfloat16)  19.1 us
    dot_general x1, matrix products, shards(): jnp.dot(new_basis, lax.all_gather(direction, 'row', axis=1, tiled=True),...  17.6 us
    dot_general x1, matrix products, shards(): jnp.einsum('mr,mn->rn', new_basis, gradient, preferred_element_type=jnp.f...  14 us
    reduce_scatter x1, waiting for transfers between devices, shards(): lax.psum_scatter(partial_sums.astype(jnp.bfloat16), 'row', scatter_dimens...  9.23 us
  transfers between devices with their start and end apart: 3, of which 3 were waited for; matrix products, arithmetic and copies ran while one was open for 15% of the time, Pallas kernels for 0%

commit v1 on v0

--- a/solution.py
+++ b/solution.py
@@ -33,7 +33,7 @@
     direction = (first_new / (jnp.sqrt(second_new) + epsilon)).astype(jnp.bfloat16)
     back = jnp.dot(
         new_basis,
-        lax.all_gather(direction, "row", axis=1, tiled=True),
+        jnp.concatenate(lax.all_gather(direction, "row"), axis=1),
         preferred_element_type=jnp.float32,
     )
     new_weight = (weight.astype(jnp.float32) - step_rate * back).astype(jnp.bfloat16)

time: 181 us -> 187 us (1.033)
  local copies, waits for them, and re-layouts: 36.9 us -> 43.1 us
    all_gather x0 -> x1, local copies, waits for them, and re-layouts: none -> 6.19 us  [shards(): lax.all_gather(direction, 'row')]
  transfers between devices with their start and end apart: 3 -> 3, of which waited for: 3 -> 3; matrix products, arithmetic and copies ran while one was open for 15% -> 14% of each run, Pallas kernels for 0% -> 0%
where the time goes in v1:
time: 187 us; the launch traced here: 186 us
  waiting for transfers between devices  66.9 us (36%)
  local copies, waits for them, and re-layouts  43.1 us (23%)
  matrix products  41.3 us (22%)
  blocking collectives  19.1 us (10%)
  between operations  15.5 us (8%)
    unnamed x13, local copies, waits for them, and re-layouts  36.9 us
    all_gather x1, waiting for transfers between devices, shards(): lax.all_gather(lax.psum(local_term, 'row').astype(jnp.bfloat16), 'col', a...  35.5 us
    all_gather x1, waiting for transfers between devices, shards(): lax.all_gather(direction, 'row')  22.1 us
    psum x1, blocking collectives, shards(): lax.psum(local_term, 'row').astype(jnp.bfloat16)  19.1 us
    dot_general x1, matrix products, shards(): jnp.dot(new_basis, jnp.concatenate(lax.all_gather(direction, 'row'), axis...  17.2 us
    dot_general x1, matrix products, shards(): jnp.einsum('mr,mn->rn', new_basis, gradient, preferred_element_type=jnp.f...  14 us
    reduce_scatter x1, waiting for transfers between devices, shards(): lax.psum_scatter(partial_sums.astype(jnp.bfloat16), 'row', scatter_dimens...  9.23 us
    all_gather x1, local copies, waits for them, and re-layouts, shards(): lax.all_gather(direction, 'row')  6.19 us
  transfers between devices with their start and end apart: 3, of which 3 were waited for; matrix products, arithmetic and copies ran while one was open for 14% of the time, Pallas kernels for 0%

profile of v1, /device:TPU:0, one launch (start us, length us, event | category | flops | bytes accessed | tf_op | source)
XLA Modules:
  0.0 186.1 jit_solution(8949549009250496392)
XLA Ops:
  8.0 0.0 all-gather.4.cloned.1.call-start
  8.0 3.1 %fusion.6 = f32[128,1024]{1,0:T(8,128)S(1)} fusion(bf16[2048,1024]{1,0:T(8,128)(2,1)} %param.9, bf16[2048,1024]{1,0:T(8,128)(2,1)} %param.8, s32[]{:T(128)S(6)} %select_n.3), kind=kOutput, calls=%fused_computation.13 | convolution fusion | flops 536870912 | bytes 5242884 | tf_op jit(solution)/shard_map/mc,mr->cr/dot_general | solution.py:19
  11.2 19.1 %all-reduce.1 = bf16[128,1024]{1,0:T(8,128)(2,1)} all-reduce(f32[128,1024]{1,0:T(8,128)S(1)} %fusion.6), channel_id=1, replica_groups=mesh['row'=4,'col'=8] {'row'}, use_global_device_ids=true, to_apply=%region_0.0 | all-reduce | flops 131072 | bytes 786432 | tf_op jit(solution)/shard_map/psum | solution.py:21
  30.2 0.0 all-gather.4.cloned.1.call-update
  30.3 0.0 reduce-scatter.2.cloned.1.call-start
  30.3 14.0 %convolution_convert_fusion = bf16[1024,2048]{1,0:T(8,128)(2,1)} fusion(bf16[2048,1024]{1,0:T(8,128)(2,1)} %param.9, bf16[2048,2048]{1,0:T(8,128)(2,1)} %param.7), kind=kOutput, calls=%fused_computation.4 | convolution fusion | flops 8592031744 | bytes 16777216 | tf_op jit(solution)/shard_map/mr,mn->rn/dot_general | solution.py:15
  44.3 0.0 copy-start
  44.3 0.0 reduce-scatter.2.cloned.1.call-update
  44.3 0.2 all-gather.6.cloned.1.call-start
  44.6 35.5 %all-gather.4.cloned.1.call-done = bf16[1024,1024]{1,0:T(8,128)(2,1)} async-done(((bf16[128,1024]{1,0:T(8,128)(2,1)}), bf16[1024,1024]{1,0:T(8,128)(2,1)}) %all-gather.4.cloned.1.call-update) | async-done | bytes 2097168 | tf_op jit(solution)/shard_map/all_gather | solution.py:20
  80.1 9.2 %reduce-scatter.2.cloned.1.call-done = bf16[1024,512]{1,0:T(8,128)(2,1)} async-done(((bf16[1024,2048]{1,0:T(8,128)(2,1)}), bf16[1024,512]{1,0:T(8,128)(2,1)}) %reduce-scatter.2.cloned.1.call-update) | async-done | bytes 1048592 | tf_op jit(solution)/shard_map/reduce_scatter | solution.py:16
  89.3 0.0 copy-done
  89.3 0.0 copy-start.1
  89.3 0.0 copy-start.2
  89.3 0.0 copy-start.3
  89.3 3.3 %fusion.2 = f32[1024,512]{1,0:T(8,128)S(1)} fusion(bf16[1024,512]{1,0:T(8,128)(2,1)} %reduce-scatter.2.cloned.1.call-done, bf16[1024,1024]{1,0:T(8,128)(2,1)} %all-gather.4.cloned.1.call-done, f32[1024,512]{1,0:T(8,128)S(1)} %copy-done), kind=kOutput, calls=%fused_computation.8 | convolution fusion | flops 1080033280 | bytes 7340032 | tf_op jit(solution)/shard_map/cr,cn->rn/dot_general | solution.py:27
  92.7 0.0 copy-done.1
  92.7 0.0 copy-done.2
  92.7 0.1 copy-done.3
  92.8 0.0 copy-start.4
  92.8 3.6 %divide_convert_fusion = (bf16[1024,512]{1,0:T(8,128)(2,1)}, f32[1024,512]{1,0:T(8,128)}) fusion(f32[1024,512]{1,0:T(8,128)S(1)} %fusion.2, bf16[1024,512]{1,0:T(8,128)(2,1)S(1)} %copy-done.3, bf16[1024,1024]{1,0:T(8,128)(2,1)S(1)} %copy-done.2, f32[1024,512]{1,0:T(8,128)S(1)} %copy-done.1), kind=kOutput, calls=%fused_computation.10 | convolution fusion | flops 1077936128 | bytes 10485760 | tf_op jit(solution)/shard_map/cr,cn->rn/dot_general | solution.py:24
  96.3 0.0 copy-done.4
  96.3 0.0 all-gather.6.cloned.1.call-update
  96.4 12.4 %copy.13 = bf16[2048,2048]{0,1:T(8,128)(2,1)} copy(bf16[2048,2048]{1,0:T(8,128)(2,1)} %param.6) | data formatting | bytes 16777216 | tf_op args[0]
  108.7 22.1 %all-gather.6.cloned.1.call-done = bf16[4096,512]{1,0:T(8,128)(2,1)} async-done(((bf16[1024,512]{1,0:T(8,128)(2,1)}), bf16[4096,512]{1,0:T(8,128)(2,1)}) %all-gather.6.cloned.1.call-update) | async-done | bytes 4194320 | tf_op jit(solution)/shard_map/all_gather | solution.py:36
  130.8 6.2 %copy.14 = bf16[4,1024,512]{1,2,0:T(8,128)(2,1)} copy(bf16[4,1024,512]{2,1,0:T(8,128)(2,1)} %bitcast.18) | data formatting | bytes 8388608 | tf_op jit(solution)/shard_map/all_gather | solution.py:36
  137.0 17.2 %fusion = (bf16[2048,2048]{0,1:T(8,128)(2,1)}, bf16[2048,2048]{1,0:T(8,128)(2,1)}) fusion(bf16[2048,2048]{0,1:T(8,128)(2,1)} %copy.13, bf16[1024,2048]{0,1:T(8,128)(2,1)} %bitcast.19, bf16[2048,1024]{1,0:T(8,128)(2,1)} %param.9), kind=kOutput, calls=%fused_computation.1 | convolution fusion | flops 8610906112 | bytes 33554432 | tf_op jit(solution)/shard_map/dot_general | solution.py:34
  154.2 12.2 %copy.15 = bf16[2048,2048]{1,0:T(8,128)(2,1)} copy(bf16[2048,2048]{0,1:T(8,128)(2,1)} %get-tuple-element.14) | data formatting | bytes 16777216
  166.5 12.2 %copy.16 = bf16[2048,2048]{1,0:T(8,128)(2,1)} copy(bf16[2048,2048]{0,1:T(8,128)(2,1)} %bitcast.17) | data formatting | bytes 16777216
Async XLA Ops:
  8.0 72.1 %all-gather.4.cloned.1.call-start = ((), (), s32[]{:S(2)}) async-start(), calls=%async_computation.1 | async-start | bytes 2359296 | tf_op jit(solution)/shard_map/all_gather | solution.py:20
  30.3 59.1 %reduce-scatter.2.cloned.1.call-start = ((), (), s32[]{:S(2)}) async-start(), calls=%async_computation.2 | async-start | bytes 5242880 | tf_op jit(solution)/shard_map/reduce_scatter | solution.py:16
  44.3 45.0 %copy-start = (f32[1024,512]{1,0:T(8,128)S(1)}, f32[1024,512]{1,0:T(8,128)}, u32[]{:S(2)}) copy-start(f32[1024,512]{1,0:T(8,128)} %param.11) | copy-start | bytes 6291460
  44.3 86.5 %all-gather.6.cloned.1.call-start = ((), (), s32[]{:S(2)}) async-start(), calls=%async_computation.3 | async-start | bytes 5242880 | tf_op jit(solution)/shard_map/all_gather | solution.py:36
  89.3 3.3 %copy-start.1 = (f32[1024,512]{1,0:T(8,128)S(1)}, f32[1024,512]{1,0:T(8,128)}, u32[]{:S(2)}) copy-start(f32[1024,512]{1,0:T(8,128)} %param.10) | copy-start | bytes 6291460
  89.3 3.3 %copy-start.2 = (bf16[1024,1024]{1,0:T(8,128)(2,1)S(1)}, bf16[1024,1024]{1,0:T(8,128)(2,1)}, u32[]{:S(2)}) copy-start(bf16[1024,1024]{1,0:T(8,128)(2,1)} %all-gather.4.cloned.1.call-done) | copy-start | bytes 6291460
  89.3 3.4 %copy-start.3 = (bf16[1024,512]{1,0:T(8,128)(2,1)S(1)}, bf16[1024,512]{1,0:T(8,128)(2,1)}, u32[]{:S(2)}) copy-start(bf16[1024,512]{1,0:T(8,128)(2,1)} %reduce-scatter.2.cloned.1.call-done) | copy-start | bytes 3145732
  92.8 3.6 %copy-start.4 = (f32[1024,512]{1,0:T(8,128)}, f32[1024,512]{1,0:T(8,128)S(1)}, u32[]{:S(2)}) copy-start(f32[1024,512]{1,0:T(8,128)S(1)} %fusion.2) | copy-start | bytes 6291460
Sparse Core Ops, SparseCore 0:
  30.4 49.6 all-gather.3
Sparse Core Ops, SparseCore 1:
  44.4 44.8 reduce-scatter.1
  96.5 34.3 all-gather.5
